TPU v7x, 32 devices: a whole 2x2x4 slice. The times are simulated.
32 devices in a mesh: groups: 2 (over y), expert: 8 (over z, core), sub: 2 (over x).
Axes of the slice: x: 2, y: 2, z: 4, core: 2. Of those that a mesh axis runs over, the one named last changes fastest.
Arguments:
- latent: bfloat16 [4096, 1024], P(('groups', 'expert', 'sub')), parts along dimension 0, may hold values from -6 to 6
- routes: int32 [4096, 4], P(('groups', 'expert', 'sub')), parts along dimension 0, may hold values from 0 to 7, all different within a row; in each aligned block of 128 rows (0 to 127, 128 to 255, ...) at most 96 rows name the same one
- gates: float32 [4096, 4], P(('groups', 'expert', 'sub')), parts along dimension 0, may hold values from 0.1 to 1
- up_weight: bfloat16 [8, 1024, 2688], P('expert', None, 'sub'), may hold values from -0.1875 to 0.1875
- down_weight: bfloat16 [8, 1024, 2688], P('expert', None, 'sub'), may hold values from -0.125 to 0.125
Outputs:
- mixed: bfloat16 [4096, 1024], P(('groups', 'expert', 'sub')), parts along dimension 0
There are 2 independent parts, one for each index of `groups`. A program takes and returns all parts, laid end to end along the dimension named above; an argument that names none is the same for every part. Nothing has to cross between parts.
Inputs may be any that keep to these rules, and one draw needn't show every extreme that they name: `routes`: each token names 4 different experts; among the 128 tokens of one device no expert is named more than 96 times, a bound that some block reaches.
All inputs are finite; a program needn't handle non-finite values.
Results may differ from a plain program's by a relative error of at most 0.0058.
Values may be sent and summed in bfloat16 or wider, within the bound.
A program may use at most 128 MiB of HBM per device.

v0:
```python
import jax
import jax.numpy as jnp
from jax import lax
from jax.sharding import PartitionSpec as P


def expert_part(row_block, up_part, down_part):
    preact = jnp.dot(row_block, up_part, preferred_element_type=jnp.float32)
    active = jnp.square(jnp.maximum(preact, 0.0)).astype(jnp.bfloat16)
    return lax.dot_general(
        active, down_part, (((1,), (1,)), ((), ())), preferred_element_type=jnp.float32
    )


def local(latent, routes, gates, up_weight, down_weight):
    tokens_here, row_width = latent.shape
    top_count = routes.shape[1]
    experts = lax.axis_size("expert")
    slot_most = min(tokens_here, 3 * tokens_here * top_count // (2 * experts))
    pair_count = tokens_here * top_count
    route_ids = routes.reshape(-1)
    one_hot = (route_ids[:, None] == jnp.arange(experts, dtype=jnp.int32)[None, :]).astype(
        jnp.int32
    )
    before = jnp.cumsum(one_hot, axis=0) - one_hot
    slot_rank = jnp.sum(before * one_hot, axis=1)
    slot_of = route_ids * slot_most + slot_rank
    source = (
        jnp.full((experts * slot_most,), pair_count, jnp.int32)
        .at[slot_of]
        .set(jnp.arange(pair_count, dtype=jnp.int32))
    )
    padded = jnp.concatenate([latent, jnp.zeros((1, row_width), latent.dtype)], axis=0)
    send_rows = padded[source // top_count].reshape(experts, slot_most, row_width)
    arrived = lax.all_to_all(send_rows, "expert", split_axis=0, concat_axis=0, tiled=True)
    flat_rows = arrived.reshape(-1, row_width)
    summed = expert_part(
        flat_rows,
        lax.all_gather(up_weight, "sub", axis=2, tiled=True)[0],
        lax.all_gather(down_weight, "sub", axis=2, tiled=True)[0],
    )
    expert_out = lax.all_to_all(
        summed.astype(jnp.bfloat16).reshape(arrived.shape),
        "expert",
        split_axis=0,
        concat_axis=0,
        tiled=True,
    )
    values = expert_out.reshape(experts * slot_most, row_width)[slot_of].astype(jnp.float32)
    mixed_out = jnp.sum(
        values.reshape(tokens_here, top_count, row_width) * gates[:, :, None], axis=1
    )
    return mixed_out.astype(jnp.bfloat16)


def solution(mesh):
    placed = (
        P(("groups", "expert", "sub"), None),
        P(("groups", "expert", "sub"), None),
        P(("groups", "expert", "sub"), None),
        P("expert", None, "sub"),
        P("expert", None, "sub"),
    )
    return jax.shard_map(
        local,
        mesh=mesh,
        in_specs=placed,
        out_specs=P(("groups", "expert", "sub"), None),
        check_vma=False,
    )
```

profile of v0, /device:TPU:0, one launch (start us, length us, event | category | flops | bytes accessed | tf_op | source)
XLA Modules:
  0.0 220.0 jit_solution(8751266270399759051)
XLA Ops:
  6.5 0.0 copy-start.1
  6.5 0.0 copy-start
  6.5 0.0 all-gather.3.cloned.1.call-start
  6.5 0.7 all-gather.3.cloned.1.call-update
  7.3 0.0 all-gather.5.cloned.1.call-start
  7.3 0.7 all-gather.5.cloned.1.call-update
  8.0 0.0 copy-done.1
  8.0 0.1 copy.8
  8.1 0.1 eq.29
  8.2 0.1 eq.25
  8.4 1.1 reduce-window.6
  9.5 0.2 slice_reduce_fusion
  9.8 0.1 copy.7
  9.9 0.1 mul.29
  10.0 0.0 copy-done
  10.0 0.1 fusion.7
  10.1 2.4 %scatter_custom_fusion = s32[768]{0:T(1024)S(1)} fusion(s32[512]{0:T(512)S(1)} %bitcast.27, s32[512]{0:T(512)S(1)} %iota.11, s32[]{:T(128)} %constant.13.clone.1), kind=kCustom, calls=%fused_computation.27 | custom fusion | bytes 3076 | tf_op jit(solution)/shard_map/scatter | solution.py:31
  12.6 2.8 %gather_fusion = bf16[768,1024]{1,0:T(8,128)(2,1)S(1)} fusion(bf16[129,1024]{1,0:T(8,128)(2,1)S(1)} %concatenate.3, s32[1024]{0:T(1024)S(1)} %pad_clamp_fusion.1), kind=kCustom, calls=%fused_computation | custom fusion | bytes 3148800 | tf_op jit(solution)/shard_map/gather | solution.py:34
  15.5 43.9 %all_to_all.10 = bf16[8,96,1024]{2,1,0:T(8,128)(2,1)S(1)} all-to-all(bf16[8,96,1024]{2,1,0:T(8,128)(2,1)S(1)} %bitcast.25), channel_id=1, replica_groups=mesh['groups'=2,'expert'=8,'sub'=2] {'expert'}, dimensions={0} | all-to-all | bytes 3145728 | tf_op jit(solution)/shard_map/all_to_all | solution.py:35
  59.4 23.7 %all-gather.3.cloned.1.call-done = bf16[1,1024,2688]{1,2,0:T(8,128)(2,1)} async-done(((bf16[1,1024,1344]{1,2,0:T(8,128)(2,1)}), bf16[1,1024,2688]{1,2,0:T(8,128)(2,1)}) %all-gather.3.cloned.1.call-update) | async-done | bytes 5505040 | tf_op jit(solution)/shard_map/all_gather | solution.py:39
  83.1 8.8 %multiply_convert_fusion = bf16[768,2688]{1,0:T(8,128)(2,1)} fusion(bf16[768,1024]{1,0:T(8,128)(2,1)S(1)} %bitcast.26, bf16[1,1024,2688]{1,2,0:T(8,128)(2,1)} %all-gather.3.cloned.1.call-done), kind=kOutput, calls=%fused_computation.3 | convolution fusion | flops 4234051584 | bytes 11206656 | tf_op jit(solution)/shard_map/dot_general | solution.py:8
  91.9 64.3 %all-gather.5.cloned.1.call-done = bf16[1,1024,2688]{1,2,0:T(8,128)(2,1)} async-done(((bf16[1,1024,1344]{1,2,0:T(8,128)(2,1)}), bf16[1,1024,2688]{1,2,0:T(8,128)(2,1)}) %all-gather.5.cloned.1.call-update) | async-done | bytes 5505040 | tf_op jit(solution)/shard_map/all_gather | solution.py:40
  156.2 9.6 %fusion.3 = bf16[768,1024]{1,0:T(8,128)(2,1)} fusion(bf16[768,2688]{1,0:T(8,128)(2,1)} %multiply_convert_fusion, bf16[1,1024,2688]{1,2,0:T(8,128)(2,1)} %all-gather.5.cloned.1.call-done), kind=kOutput, calls=%fused_computation.8 | convolution fusion | flops 4228644864 | bytes 11206656 | tf_op jit(solution)/shard_map/dot_general | solution.py:10
  165.8 0.0 copy-start.2
  165.8 4.7 %all-to-all-start.1 = ((bf16[8,96,1024]{2,1,0:T(8,128)(2,1)}), bf16[8,96,1024]{2,1,0:T(8,128)(2,1)S(1)}, u32[]{:S(2)}, u32[]{:S(2)}) async-start(bf16[8,96,1024]{2,1,0:T(8,128)(2,1)} %bitcast.8), calls=%async_computation.1 | async-start | bytes 3145728 | tf_op jit(solution)/shard_map/all_to_all | solution.py:42
  170.6 0.0 copy-done.2
  170.6 0.1 copy.10
  170.7 37.7 %all-to-all-done.1 = bf16[8,96,1024]{2,1,0:T(8,128)(2,1)S(1)} async-done(((bf16[8,96,1024]{2,1,0:T(8,128)(2,1)}), bf16[8,96,1024]{2,1,0:T(8,128)(2,1)S(1)}, u32[]{:S(2)}, u32[]{:S(2)}) %all-to-all-start.1) | async-done | bytes 1572896 | tf_op jit(solution)/shard_map/all_to_all | solution.py:42
  208.4 2.0 gather_fusion.1
  210.4 0.7 reshape.68
  211.1 2.1 multiply_reduce_fusion
  (10 shorter events, 0.1 us)
Async XLA Ops:
  6.5 1.5 copy-start.1
  6.5 3.5 %copy-start = (bf16[128,1024]{1,0:T(8,128)(2,1)S(1)}, bf16[128,1024]{1,0:T(8,128)(2,1)}, u32[]{:S(2)}) copy-start(bf16[128,1024]{1,0:T(8,128)(2,1)} %param.5) | copy-start | bytes 786436
  6.5 76.6 %all-gather.3.cloned.1.call-start = ((), (), s32[]{:S(2)}) async-start(), calls=%async_computation.2 | async-start | bytes 8257536 | tf_op jit(solution)/shard_map/all_gather | solution.py:39
  7.3 149.0 %all-gather.5.cloned.1.call-start = ((), (), s32[]{:S(2)}) async-start(), calls=%async_computation.3 | async-start | bytes 8257536 | tf_op jit(solution)/shard_map/all_gather | solution.py:40
  165.8 4.7 %copy-start.2 = (f32[128,4]{0,1:T(4,128)S(1)}, f32[128,4]{0,1:T(4,128)}, u32[]{:S(2)}) copy-start(f32[128,4]{0,1:T(4,128)} %param.7) | copy-start | bytes 6148
  165.8 42.5 %all-to-all-start.1 = ((bf16[8,96,1024]{2,1,0:T(8,128)(2,1)}), bf16[8,96,1024]{2,1,0:T(8,128)(2,1)S(1)}, u32[]{:S(2)}, u32[]{:S(2)}) async-start(bf16[8,96,1024]{2,1,0:T(8,128)(2,1)} %bitcast.8), calls=%async_computation.1 | async-start | bytes 3145728 | tf_op jit(solution)/shard_map/all_to_all | solution.py:42
Sparse Core Ops, SparseCore 0:
  8.9 74.2 all-gather.2
  84.7 71.4 all-gather.4
where the time goes:
time: 220 us
  waiting for transfers between devices  127 us (58%)
  blocking collectives  43.9 us (20%)
  matrix products  18.4 us (8%)
  between operations  13.5 us (6%)
  local copies, waits for them, and re-layouts  8.93 us (4%)
  starting transfers between devices  4.78 us (2%)
  other arithmetic  3.39 us (2%)
    all_gather x1, waiting for transfers between devices, local(): lax.all_gather(down_weight, 'sub', axis=2, tiled=True)[0]  64.3 us
    all_to_all x1, blocking collectives, local(): lax.all_to_all(send_rows, 'expert', split_axis=0, concat_axis=0, tiled=True)  43.9 us
    all_to_all x1, waiting for transfers between devices, local(): lax.all_to_all(summed.astype(jnp.bfloat16).reshape(arrived.shape), 'exper...  37.7 us
    all_gather x1, waiting for transfers between devices, local(): lax.all_gather(up_weight, 'sub', axis=2, tiled=True)[0]  23.7 us
    dot_general x1, matrix products, expert_part(): lax.dot_general(active, down_part, (((1,), (1,)), ((), ())), preferred_el...  9.62 us
    dot_general x1, matrix products, expert_part(): preact = jnp.dot(row_block, up_part, preferred_element_type=jnp.float32)  8.77 us
    all_to_all x1, starting transfers between devices, local(): lax.all_to_all(summed.astype(jnp.bfloat16).reshape(arrived.shape), 'exper...  4.74 us
  transfers between devices with their start and end apart: 3, of which 3 were waited for; matrix products, arithmetic and copies ran while one was open for 7% of the time, Pallas kernels for 0%

commit v1 on v0

v1 whole, which is shorter than its diff:
```python
import jax
import jax.numpy as jnp
from jax import lax
from jax.sharding import PartitionSpec as P

TEAM = ("expert", "sub")


def local(latent, routes, gates, up_weight, down_weight):
    experts = lax.axis_size("expert")
    chosen = routes[:, :, None] == jnp.arange(experts, dtype=jnp.int32)[None, None, :]
    share = jnp.sum(jnp.where(chosen, gates[:, :, None], 0.0), axis=1)
    rows = lax.all_gather(latent, TEAM, axis=0, tiled=True)
    shares = lax.all_gather(share, TEAM, axis=0, tiled=True)
    mine = lax.axis_index("expert")
    weight = jnp.sum(
        jnp.where(jnp.arange(experts)[None, :] == mine, shares, 0.0), axis=1, keepdims=True
    )
    preact = jnp.dot(rows, up_weight[0], preferred_element_type=jnp.float32)
    active = jnp.square(jnp.maximum(preact, 0.0)).astype(jnp.bfloat16)
    part = lax.dot_general(
        active, down_weight[0], (((1,), (1,)), ((), ())), preferred_element_type=jnp.float32
    )
    part = (part * weight).astype(jnp.bfloat16)
    return lax.psum_scatter(part, TEAM, scatter_dimension=0, tiled=True)


def solution(mesh):
    placed = (
        P(("groups", "expert", "sub"), None),
        P(("groups", "expert", "sub"), None),
        P(("groups", "expert", "sub"), None),
        P("expert", None, "sub"),
        P("expert", None, "sub"),
    )
    return jax.shard_map(
        local,
        mesh=mesh,
        in_specs=placed,
        out_specs=P(("groups", "expert", "sub"), None),
        check_vma=False,
    )
```

time: 220 us -> 159 us (0.72)
  waiting for transfers between devices: 127 us -> 92.3 us
  blocking collectives: 43.9 us -> 34.6 us
  local copies, waits for them, and re-layouts: 8.93 us -> 0.01 us
  starting transfers between devices: 4.78 us -> 0.04 us
  other arithmetic: 3.39 us -> 0.86 us
    reduce_scatter x0 -> x1, waiting for transfers between devices: none -> 71.4 us  [local(): return lax.psum_scatter(part, TEAM, scatter_dimension=0, tiled=True)]
    all_gather x2 -> x1, waiting for transfers between devices: 88 us -> 20.1 us  [local(): rows = lax.all_gather(latent, TEAM, axis=0, tiled=True)]
    all_to_all x1 -> x0, blocking collectives: 43.9 us -> none  [local(): lax.all_to_all(send_rows, 'expert', split_axis=0, concat_axis=0, tiled=True)]
    all_to_all x1 -> x0, waiting for transfers between devices: 37.7 us -> none  [local(): lax.all_to_all(summed.astype(jnp.bfloat16).reshape(arrived.shape), 'exper...]
    all_gather x0 -> x1, blocking collectives: none -> 34.6 us  [local(): shares = lax.all_gather(share, TEAM, axis=0, tiled=True)]
    gather x2 -> x0, local copies, waits for them, and re-layouts: 4.86 us -> none  [the longest x1 2.81 us: local(): padded[source // top_count].reshape(experts, slot_most, row_width)]
    all_to_all x1 -> x0, starting transfers between devices: 4.74 us -> none  [local(): lax.all_to_all(summed.astype(jnp.bfloat16).reshape(arrived.shape), 'exper...]
    scatter x1 -> x0, local copies, waits for them, and re-layouts: 2.45 us -> none  [local(): source = jnp.full((experts * slot_most,), pair_count, jnp.int32).at[slot_...]
  transfers between devices with their start and end apart: 3 -> 2, of which waited for: 3 -> 2; matrix products, arithmetic and copies ran while one was open for 7% -> 1% of each run, Pallas kernels for 0% -> 0%
where the time goes in v1:
time: 159 us; the launch traced here: 158 us
  waiting for transfers between devices  92.3 us (58%)
  blocking collectives  34.6 us (22%)
  matrix products  17.2 us (11%)
  between operations  13.4 us (8%)
    reduce_scatter x1, waiting for transfers between devices, local(): return lax.psum_scatter(part, TEAM, scatter_dimension=0, tiled=True)  71.4 us
    all_gather x1, blocking collectives, local(): shares = lax.all_gather(share, TEAM, axis=0, tiled=True)  34.6 us
    all_gather x1, waiting for transfers between devices, local(): rows = lax.all_gather(latent, TEAM, axis=0, tiled=True)  20.1 us
    dot_general x1, matrix products, local(): lax.dot_general(active, down_weight[0], (((1,), (1,)), ((), ())), preferr...  17.2 us
  transfers between devices with their start and end apart: 2, of which 2 were waited for; matrix products, arithmetic and copies ran while one was open for 1% of the time, Pallas kernels for 0%

profile of v1, /device:TPU:0, one launch (start us, length us, event | category | flops | bytes accessed | tf_op | source)
XLA Modules:
  0.0 158.4 jit_solution(11890583778137801550)
XLA Ops:
  6.5 0.0 copy-start
  6.5 0.0 all-gather.2.cloned.1.call-start
  6.5 0.7 all-gather.2.cloned.1.call-update
  7.3 0.0 reduce-scatter.2.cloned.1.call-start
  7.3 0.8 select_reduce_fusion.1
  8.1 34.6 %all_gather.7 = f32[2048,8]{0,1:T(8,128)S(1)} all-gather(f32[128,8]{0,1:T(8,128)S(1)} %select_reduce_fusion.1), channel_id=1, replica_groups=mesh['groups'=2,'expert'=8,'sub'=2] {'expert','sub'}, dimensions={0}, use_global_device_ids=true | all-gather | bytes 69632 | tf_op jit(solution)/shard_map/all_gather | solution.py:14
  42.7 0.1 select_reduce_fusion
  42.8 20.1 %all-gather.2.cloned.1.call-done = bf16[2048,1024]{1,0:T(8,128)(2,1)} async-done(((bf16[128,1024]{1,0:T(8,128)(2,1)}), bf16[2048,1024]{1,0:T(8,128)(2,1)}) %all-gather.2.cloned.1.call-update) | async-done | bytes 4194320 | tf_op jit(solution)/shard_map/all_gather | solution.py:13
  62.9 0.0 copy-done
  62.9 17.2 %multiply_convert_fusion.1 = bf16[2048,1024]{1,0:T(8,128)(2,1)} fusion(f32[2048]{0:T(1024)S(1)} %select_reduce_fusion, bf16[1,1024,1344]{1,2,0:T(8,128)(2,1)S(1)} %copy-done, bf16[2048,1024]{1,0:T(8,128)(2,1)} %all-gather.2.cloned.1.call-done, bf16[1,1024,1344]{1,2,0:T(8,128)(2,1)} %param.8), kind=kOutput, calls=%fused_computation.1 | convolution fusion | flops 11286740992 | bytes 13901824 | tf_op jit(solution)/shard_map/dot_general | solution.py:21
  80.1 0.0 reduce-scatter.2.cloned.1.call-update
  80.1 71.4 %reduce-scatter.2.cloned.1.call-done = bf16[128,1024]{1,0:T(8,128)(2,1)} async-done(((bf16[2048,1024]{1,0:T(8,128)(2,1)}), bf16[128,1024]{1,0:T(8,128)(2,1)}) %reduce-scatter.2.cloned.1.call-update) | async-done | bytes 262160 | tf_op jit(solution)/shard_map/reduce_scatter | solution.py:25
  (1 shorter events, 0.0 us)
Async XLA Ops:
  6.5 56.4 %copy-start = (bf16[1,1024,1344]{1,2,0:T(8,128)(2,1)S(1)}, bf16[1,1024,1344]{1,2,0:T(8,128)(2,1)}, u32[]{:S(2)}) copy-start(bf16[1,1024,1344]{1,2,0:T(8,128)(2,1)} %param.9) | copy-start | bytes 8257540
  6.5 56.4 %all-gather.2.cloned.1.call-start = ((), (), s32[]{:S(2)}) async-start(), calls=%async_computation.1 | async-start | bytes 4456448 | tf_op jit(solution)/shard_map/all_gather | solution.py:13
  7.3 144.3 %reduce-scatter.2.cloned.1.call-start = ((), (), s32[]{:S(2)}) async-start(), calls=%async_computation.2 | async-start | bytes 4456448 | tf_op jit(solution)/shard_map/reduce_scatter | solution.py:25
Sparse Core Ops, SparseCore 0:
  9.5 53.3 all-gather.1
  80.2 71.2 reduce-scatter.1

commit v2 on v0

--- a/solution.py
+++ b/solution.py
@@ -1,18 +1,26 @@
+import functools
+
 import jax
 import jax.numpy as jnp
 from jax import lax
+from jax.experimental import pallas as pl
+from jax.experimental.pallas import tpu as pltpu
 from jax.sharding import PartitionSpec as P
 
+CORES = 2
+VMEM_MOST = 60 * 1024 * 1024
+F32, BF16 = jnp.float32, jnp.bfloat16
+
 
 def expert_part(row_block, up_part, down_part):
-    preact = jnp.dot(row_block, up_part, preferred_element_type=jnp.float32)
-    active = jnp.square(jnp.maximum(preact, 0.0)).astype(jnp.bfloat16)
+    preact = jnp.dot(row_block, up_part, preferred_element_type=F32)
+    active = jnp.square(jnp.maximum(preact, 0.0)).astype(BF16)
     return lax.dot_general(
-        active, down_part, (((1,), (1,)), ((), ())), preferred_element_type=jnp.float32
-    )
-
-
-def local(latent, routes, gates, up_weight, down_weight):
+        active, down_part, (((1,), (1,)), ((), ())), preferred_element_type=F32
+    )
+
+
+def routed(latent, routes, gates, up_weight, down_weight):
     tokens_here, row_width = latent.shape
     top_count = routes.shape[1]
     experts = lax.axis_size("expert")
@@ -40,17 +48,222 @@
         lax.all_gather(down_weight, "sub", axis=2, tiled=True)[0],
     )
     expert_out = lax.all_to_all(
-        summed.astype(jnp.bfloat16).reshape(arrived.shape),
+        summed.astype(BF16).reshape(arrived.shape),
         "expert",
         split_axis=0,
         concat_axis=0,
         tiled=True,
     )
-    values = expert_out.reshape(experts * slot_most, row_width)[slot_of].astype(jnp.float32)
+    values = expert_out.reshape(experts * slot_most, row_width)[slot_of].astype(F32)
     mixed_out = jnp.sum(
         values.reshape(tokens_here, top_count, row_width) * gates[:, :, None], axis=1
     )
-    return mixed_out.astype(jnp.bfloat16)
+    return mixed_out.astype(BF16)
+
+
+def team_kernel(
+    lanes,
+    latent_ref, share_ref, up_hbm, down_hbm, out_ref,
+    rows, shares, up, down, kept, sib_out, sib_in, x_out, x_in, lane_out, lane_in,
+    w_sem, lane_s, lane_r, x_s, x_r, sib_s, sib_r,
+    rsib_s, rsib_r, rx_s, rx_r, rlane_s, rlane_r,
+):
+    tokens = latent_ref.shape[0]
+    me = lax.axis_index("expert")
+    sub = lax.axis_index("sub")
+    chip, core = me // CORES, me % CORES
+    sibling = {"expert": chip * CORES + 1 - core}
+    partner = {"sub": 1 - sub}
+    bits = lanes.bit_length() - 1
+
+    def lane_peer(step):
+        place = 0
+        for bit in range(bits):
+            size = 1 << bit
+            place = place + size * ((chip // size + step // size) % 2)
+        return {"expert": place * CORES + core}
+
+    def send(src, dst, s_sem, r_sem, device):
+        return pltpu.make_async_remote_copy(
+            src_ref=src, dst_ref=dst, send_sem=s_sem, recv_sem=r_sem,
+            device_id=device, device_id_type=pl.DeviceIdType.MESH,
+        )
+
+    own = (latent_ref, share_ref)
+    boxes = (rows, shares)
+
+    def to_lane(kind, step):
+        return send(own[kind], boxes[kind].at[0, step, 0], lane_s.at[kind, step],
+                    lane_r.at[kind, step], lane_peer(step))
+
+    def to_sub(kind, step, src=None):
+        src = boxes[kind].at[0, step, 0] if src is None else src
+        return send(src, boxes[kind].at[1, step, 0], x_s.at[kind, step],
+                    x_r.at[kind, step], partner)
+
+    def to_sibling(kind, other, step, src=None):
+        src = boxes[kind].at[other, step, 0] if src is None else src
+        return send(src, boxes[kind].at[other, step, 1], sib_s.at[kind, other, step],
+                    sib_r.at[kind, other, step], sibling)
+
+    def back_sibling(other, step):
+        return send(sib_out.at[other, step], sib_in.at[other, step], rsib_s.at[other, step],
+                    rsib_r.at[other, step], sibling)
+
+    def back_sub(step):
+        return send(x_out.at[step], x_in.at[step], rx_s.at[step], rx_r.at[step], partner)
+
+    def back_lane(step):
+        return send(lane_out.at[step], lane_in.at[step], rlane_s.at[step],
+                    rlane_r.at[step], lane_peer(step))
+
+    up_copy = pltpu.make_async_copy(up_hbm.at[0], up, w_sem.at[0])
+    down_copy = pltpu.make_async_copy(down_hbm.at[0], down, w_sem.at[1])
+    up_copy.start()
+    down_copy.start()
+
+    barrier = pltpu.get_barrier_semaphore()
+    greeted = [sibling, partner] + [lane_peer(step) for step in range(1, lanes)]
+    for device in greeted:
+        pl.semaphore_signal(barrier, inc=1, device_id=device,
+                            device_id_type=pl.DeviceIdType.MESH)
+    pl.semaphore_wait(barrier, len(greeted))
+
+    for kind in (1, 0):
+        to_sub(kind, 0, own[kind]).start()
+        to_sibling(kind, 0, 0, own[kind]).start()
+        for step in range(1, lanes):
+            to_lane(kind, step).start()
+    rows[0, 0, 0] = latent_ref[...]
+    shares[0, 0, 0] = share_ref[...]
+    up_copy.wait()
+    down_copy.wait()
+
+    def finish_sub(step):
+        back_sibling(1, step).wait_recv()
+        total = kept[1, step] + sib_in[1, step].astype(F32)
+        x_out[step] = total.astype(BF16)
+        back_sub(step).start()
+
+    def gate_column(other, step, side):
+        line = shares[other, step, side, me]
+        spot = lax.broadcasted_iota(jnp.int32, (tokens, tokens), 0) == lax.broadcasted_iota(
+            jnp.int32, (tokens, tokens), 1
+        )
+        return jnp.sum(jnp.where(spot, line, 0.0), axis=1, keepdims=True)
+
+    def one(index, carry):
+        step, other = index // 2, index % 2
+
+        @pl.when((other == 1) & (step + 1 < lanes))
+        def _():
+            for kind in (0, 1):
+                to_lane(kind, step + 1).wait_recv()
+                to_sub(kind, step + 1).start()
+                to_sibling(kind, 0, step + 1).start()
+
+        @pl.when(other == 1)
+        def _():
+            for kind in (0, 1):
+                to_sub(kind, step).wait_recv()
+                to_sibling(kind, 1, step).start()
+
+        for kind in (0, 1):
+            to_sibling(kind, other, step).wait_recv()
+        block = rows[other, step].reshape(2 * tokens, rows.shape[-1])
+        part = expert_part(block, up[...], down[...])
+        kept[other, step] = part[:tokens] * gate_column(other, step, 0)
+        sib_out[other, step] = (part[tokens:] * gate_column(other, step, 1)).astype(BF16)
+        back_sibling(other, step).start()
+
+        @pl.when((other == 0) & (step >= 2))
+        def _():
+            finish_sub(step - 1)
+
+        return carry
+
+    lax.fori_loop(0, 2 * lanes, one, 0)
+
+    if lanes > 1:
+        finish_sub(lanes - 1)
+    finish_sub(0)
+
+    def column_total(step):
+        back_sibling(0, step).wait_recv()
+        back_sub(step).wait_recv()
+        return kept[0, step] + sib_in[0, step].astype(F32) + x_in[step].astype(F32)
+
+    for step in range(1, lanes):
+        lane_out[step] = column_total(step).astype(BF16)
+        back_lane(step).start()
+    total = column_total(0)
+    for step in range(1, lanes):
+        back_lane(step).wait_recv()
+        total = total + lane_in[step].astype(F32)
+    out_ref[...] = total.astype(BF16)
+
+    for step in range(lanes):
+        for kind in (0, 1):
+            to_sub(kind, step).wait_send()
+            for other in (0, 1):
+                to_sibling(kind, other, step).wait_send()
+            if step:
+                to_lane(kind, step).wait_send()
+        for other in (0, 1):
+            back_sibling(other, step).wait_send()
+        back_sub(step).wait_send()
+        if step:
+            back_lane(step).wait_send()
+
+
+def team(latent, routes, gates, up_weight, down_weight):
+    tokens, width = latent.shape
+    hidden = up_weight.shape[2]
+    experts = lax.axis_size("expert")
+    lanes = experts // CORES
+    chosen = routes[None, :, :] == jnp.arange(experts, dtype=jnp.int32)[:, None, None]
+    share = jnp.sum(jnp.where(chosen, gates[None, :, :], 0.0), axis=2).reshape(experts, 1, tokens)
+    vmem = pl.BlockSpec(memory_space=pltpu.VMEM)
+    hbm = pl.BlockSpec(memory_space=pl.ANY)
+    dma = pltpu.SemaphoreType.DMA
+    return pl.pallas_call(
+        functools.partial(team_kernel, lanes),
+        out_shape=jax.ShapeDtypeStruct((tokens, width), BF16),
+        in_specs=[vmem, vmem, hbm, hbm],
+        out_specs=vmem,
+        scratch_shapes=[
+            pltpu.VMEM((2, lanes, 2, tokens, width), BF16),
+            pltpu.VMEM((2, lanes, 2, experts, 1, tokens), F32),
+            pltpu.VMEM((width, hidden), BF16),
+            pltpu.VMEM((width, hidden), BF16),
+            pltpu.VMEM((2, lanes, tokens, width), F32),
+            pltpu.VMEM((2, lanes, tokens, width), BF16),
+            pltpu.VMEM((2, lanes, tokens, width), BF16),
+            pltpu.VMEM((lanes, tokens, width), BF16),
+            pltpu.VMEM((lanes, tokens, width), BF16),
+            pltpu.VMEM((lanes, tokens, width), BF16),
+            pltpu.VMEM((lanes, tokens, width), BF16),
+            dma((2,)),
+            dma((2, lanes)), dma((2, lanes)), dma((2, lanes)), dma((2, lanes)),
+            dma((2, 2, lanes)), dma((2, 2, lanes)),
+            dma((2, lanes)), dma((2, lanes)),
+            dma((lanes,)), dma((lanes,)), dma((lanes,)), dma((lanes,)),
+        ],
+        compiler_params=pltpu.CompilerParams(
+            collective_id=0, has_side_effects=True, vmem_limit_bytes=VMEM_MOST
+        ),
+    )(latent, share, up_weight, down_weight)
+
+
+def local(latent, routes, gates, up_weight, down_weight):
+    tokens, width = latent.shape
+    experts, subs = lax.axis_size("expert"), lax.axis_size("sub")
+    lanes = experts // CORES
+    block = tokens * width * 2
+    need = block * lanes * (4 + 4 + 2 + 2 + 4) + 4 * up_weight.size + 16 * block
+    fits = subs == 2 and lanes & (lanes - 1) == 0 and need < VMEM_MOST
+    plan = team if fits and experts % CORES == 0 and tokens % 128 == 0 else routed
+    return plan(latent, routes, gates, up_weight, down_weight)
 
 
 def solution(mesh):

time: 220 us -> 81.7 us (0.37)
  waiting for transfers between devices: 127 us -> 0 us
  Pallas kernels: 0 us -> 71 us
  blocking collectives: 43.9 us -> 0 us
  matrix products: 18.4 us -> 0 us
  between operations: 13.5 us -> 0.01 us
  starting transfers between devices: 4.78 us -> 0 us
    all_gather x2 -> x0, waiting for transfers between devices: 88 us -> none  [the longest x1 64.3 us: local(): lax.all_gather(down_weight, 'sub', axis=2, tiled=True)[0]]
    pallas_call x0 -> x1, Pallas kernels: none -> 71 us  [team(): pl.pallas_call(functools.partial(team_kernel, lanes), out_shape=jax.Shape...]
    all_to_all x1 -> x0, blocking collectives: 43.9 us -> none  [local(): lax.all_to_all(send_rows, 'expert', split_axis=0, concat_axis=0, tiled=True)]
    all_to_all x1 -> x0, waiting for transfers between devices: 37.7 us -> none  [local(): lax.all_to_all(summed.astype(jnp.bfloat16).reshape(arrived.shape), 'exper...]
    dot_general x2 -> x0, matrix products: 18.4 us -> none  [the longest x1 9.62 us: expert_part(): lax.dot_general(active, down_part, (((1,), (1,)), ((), ())), preferred_el...]
    unnamed x8 -> x5, local copies, waits for them, and re-layouts: 0.24 us -> 9.06 us
    gather x2 -> x0, local copies, waits for them, and re-layouts: 4.86 us -> none  [the longest x1 2.81 us: local(): padded[source // top_count].reshape(experts, slot_most, row_width)]
    all_to_all x1 -> x0, starting transfers between devices: 4.74 us -> none  [local(): lax.all_to_all(summed.astype(jnp.bfloat16).reshape(arrived.shape), 'exper...]
  transfers between devices with their start and end apart: 3 -> 0, of which waited for: 3 -> 0; matrix products, arithmetic and copies ran while one was open for 7% -> 0% of each run, Pallas kernels for 0% -> 0%
where the time goes in v2:
time: 81.7 us; the launch traced here: 81.5 us
  Pallas kernels  71 us (87%)
  local copies, waits for them, and re-layouts  9.06 us (11%)
  other arithmetic  1.45 us (2%)
    pallas_call x1, Pallas kernels, team(): pl.pallas_call(functools.partial(team_kernel, lanes), out_shape=jax.Shape...  71 us
    unnamed x5, local copies, waits for them, and re-layouts  9.06 us

profile of v2, /device:TPU:0, one launch (start us, length us, event | category | flops | bytes accessed | tf_op | source)
XLA Modules:
  0.0 81.5 jit_solution(15106216189245980830)
XLA Ops:
  0.0 0.0 copy-start
  0.0 1.4 %select_reduce_fusion = f32[8,128]{1,0:T(8,128)} fusion(f32[128,4]{0,1:T(4,128)} %param.7, s32[128,4]{0,1:T(4,128)} %param.6), kind=kLoop, calls=%fused_computation | loop fusion | flops 11264 | bytes 8192 | tf_op jit(solution)/shard_map/reduce_sum | solution.py:225
  1.5 4.5 %copy.10.up_hbm = bf16[1,1024,1344]{2,1,0:T(8,128)(2,1)} copy(bf16[1,1024,1344]{1,2,0:T(8,128)(2,1)} %param.8) | data formatting | bytes 5505024 | tf_op args[3]
  6.0 0.0 copy-done
  6.0 2.9 %copy.11.down_hbm = bf16[1,1024,1344]{2,1,0:T(8,128)(2,1)} copy(bf16[1,1024,1344]{1,2,0:T(8,128)(2,1)S(1)} %copy-done) | data formatting | bytes 5505024 | tf_op args[4]
  8.8 71.0 %shard_map.55 = bf16[128,1024]{1,0:T(8,128)(2,1)} custom-call(bf16[128,1024]{1,0:T(8,128)(2,1)} %latent_ref.1, f32[8,1,128]{2,1,0:T(1,128)} %bitcast.1, bf16[1,1024,1344]{2,1,0:T(8,128)(2,1)} %copy.10.up_hbm, bf16[1,1024,1344]{2,1,0:T(8,128)(2,1)} %copy.11.down_hbm), custom_call_target="tpu_custom_call" | custom-call | tf_op jit(solution)/shard_map/pallas_call | solution.py:229
  79.8 1.7 %copy.13 = bf16[128,1024]{1,0:T(8,128)(2,1)} copy(bf16[128,1024]{1,0:T(8,128)(2,1)} %shard_map.55) | data formatting | bytes 524288
Async XLA Ops:
  0.0 6.0 %copy-start = (bf16[1,1024,1344]{1,2,0:T(8,128)(2,1)S(1)}, bf16[1,1024,1344]{1,2,0:T(8,128)(2,1)}, u32[]{:S(2)}) copy-start(bf16[1,1024,1344]{1,2,0:T(8,128)(2,1)} %param.9) | copy-start | bytes 8257540

commit v3 on v2

--- a/solution.py
+++ b/solution.py
@@ -92,9 +92,22 @@
     own = (latent_ref, share_ref)
     boxes = (rows, shares)
 
-    def to_lane(kind, step):
-        return send(own[kind], boxes[kind].at[0, step, 0], lane_s.at[kind, step],
-                    lane_r.at[kind, step], lane_peer(step))
+    def to_lane(kind, step, hops=None, src=None, slot=None):
+        hops = step if hops is None else hops
+        src = own[kind] if src is None else boxes[kind].at[0, src, 0]
+        slot = step if slot is None else slot
+        return send(src, boxes[kind].at[0, step, 0], lane_s.at[kind, slot],
+                    lane_r.at[kind, step], lane_peer(hops))
+
+    relay = lanes == 4
+    inner = ((chip + 1) // 2) % 2 == 1
+
+    def relayed(kind, what):
+        if what == 0:
+            return to_lane(kind, 2, 3, 1, 2)
+        if what == 1:
+            return to_lane(kind, 2, 1, 3, 4)
+        return to_lane(kind, 3, 1, 2, 5)
 
     def to_sub(kind, step, src=None):
         src = boxes[kind].at[0, step, 0] if src is None else src
@@ -132,8 +145,15 @@
     for kind in (1, 0):
         to_sub(kind, 0, own[kind]).start()
         to_sibling(kind, 0, 0, own[kind]).start()
-        for step in range(1, lanes):
-            to_lane(kind, step).start()
+        if relay:
+            to_lane(kind, 1).start()
+
+            @pl.when(inner)
+            def _():
+                to_lane(kind, 3).start()
+        else:
+            for step in range(1, lanes):
+                to_lane(kind, step).start()
     rows[0, 0, 0] = latent_ref[...]
     shares[0, 0, 0] = share_ref[...]
     up_copy.wait()
@@ -157,8 +177,28 @@
 
         @pl.when((other == 1) & (step + 1 < lanes))
         def _():
+            if relay:
+                @pl.when(jnp.logical_not(inner & (step == 2)))
+                def _():
+                    for kind in (0, 1):
+                        to_lane(kind, step + 1).wait_recv()
+
+                @pl.when(inner & (step == 0))
+                def _():
+                    for kind in (0, 1):
+                        relayed(kind, 0).start()
+                    for kind in (0, 1):
+                        to_lane(kind, 3).wait_recv()
+                        relayed(kind, 1).start()
+
+                @pl.when(inner & (step == 1))
+                def _():
+                    for kind in (0, 1):
+                        relayed(kind, 2).start()
+            else:
+                for kind in (0, 1):
+                    to_lane(kind, step + 1).wait_recv()
             for kind in (0, 1):
-                to_lane(kind, step + 1).wait_recv()
                 to_sub(kind, step + 1).start()
                 to_sibling(kind, 0, step + 1).start()
 
@@ -171,12 +211,16 @@
         for kind in (0, 1):
             to_sibling(kind, other, step).wait_recv()
         block = rows[other, step].reshape(2 * tokens, rows.shape[-1])
-        part = expert_part(block, up[...], down[...])
+        preact = lax.dot_general(
+            block, up[...], (((1,), (1,)), ((), ())), preferred_element_type=F32
+        )
+        active = jnp.square(jnp.maximum(preact, 0.0)).astype(BF16)
+        part = jnp.dot(active, down[...], preferred_element_type=F32)
         kept[other, step] = part[:tokens] * gate_column(other, step, 0)
         sib_out[other, step] = (part[tokens:] * gate_column(other, step, 1)).astype(BF16)
         back_sibling(other, step).start()
 
-        @pl.when((other == 0) & (step >= 2))
+        @pl.when((other == 0) & (step >= 3))
         def _():
             finish_sub(step - 1)
 
@@ -184,16 +228,15 @@
 
     lax.fori_loop(0, 2 * lanes, one, 0)
 
-    if lanes > 1:
-        finish_sub(lanes - 1)
-    finish_sub(0)
+    for step in (*range(min(lanes, 3) - 1, 0, -1), 0) if lanes < 4 else (lanes - 1, 1, 0):
+        finish_sub(step)
 
     def column_total(step):
         back_sibling(0, step).wait_recv()
         back_sub(step).wait_recv()
         return kept[0, step] + sib_in[0, step].astype(F32) + x_in[step].astype(F32)
 
-    for step in range(1, lanes):
+    for step in (*range(2, lanes), 1) if lanes > 1 else ():
         lane_out[step] = column_total(step).astype(BF16)
         back_lane(step).start()
     total = column_total(0)
@@ -207,13 +250,20 @@
             to_sub(kind, step).wait_send()
             for other in (0, 1):
                 to_sibling(kind, other, step).wait_send()
-            if step:
+            if step == 1 or (step and not relay):
                 to_lane(kind, step).wait_send()
         for other in (0, 1):
             back_sibling(other, step).wait_send()
         back_sub(step).wait_send()
         if step:
             back_lane(step).wait_send()
+    if relay:
+        @pl.when(inner)
+        def _():
+            for kind in (0, 1):
+                to_lane(kind, 3).wait_send()
+                for what in range(3):
+                    relayed(kind, what).wait_send()
 
 
 def team(latent, routes, gates, up_weight, down_weight):
@@ -234,8 +284,8 @@
         scratch_shapes=[
             pltpu.VMEM((2, lanes, 2, tokens, width), BF16),
             pltpu.VMEM((2, lanes, 2, experts, 1, tokens), F32),
-            pltpu.VMEM((width, hidden), BF16),
-            pltpu.VMEM((width, hidden), BF16),
+            pltpu.VMEM((hidden, width), BF16),
+            pltpu.VMEM((hidden, width), BF16),
             pltpu.VMEM((2, lanes, tokens, width), F32),
             pltpu.VMEM((2, lanes, tokens, width), BF16),
             pltpu.VMEM((2, lanes, tokens, width), BF16),
@@ -244,7 +294,7 @@
             pltpu.VMEM((lanes, tokens, width), BF16),
             pltpu.VMEM((lanes, tokens, width), BF16),
             dma((2,)),
-            dma((2, lanes)), dma((2, lanes)), dma((2, lanes)), dma((2, lanes)),
+            dma((2, lanes + 2)), dma((2, lanes)), dma((2, lanes)), dma((2, lanes)),
             dma((2, 2, lanes)), dma((2, 2, lanes)),
             dma((2, lanes)), dma((2, lanes)),
             dma((lanes,)), dma((lanes,)), dma((lanes,)), dma((lanes,)),
@@ -252,7 +302,7 @@
         compiler_params=pltpu.CompilerParams(
             collective_id=0, has_side_effects=True, vmem_limit_bytes=VMEM_MOST
         ),
-    )(latent, share, up_weight, down_weight)
+    )(latent, share, jnp.swapaxes(up_weight, 1, 2), jnp.swapaxes(down_weight, 1, 2))
 
 
 def local(latent, routes, gates, up_weight, down_weight):

time: 81.7 us -> 67.9 us (0.83)
  local copies, waits for them, and re-layouts: 9.06 us -> 1.67 us
  Pallas kernels: 71 us -> 64.7 us
    unnamed x5 -> x1, local copies, waits for them, and re-layouts: 9.06 us -> 1.67 us
    pallas_call x1, Pallas kernels: 71 us -> 64.7 us  [team(): pl.pallas_call(functools.partial(team_kernel, lanes), out_shape=jax.Shape...]
where the time goes in v3:
time: 67.9 us; the launch traced here: 67.7 us
  Pallas kernels  64.7 us (95%)
  local copies, waits for them, and re-layouts  1.67 us (2%)
  other arithmetic  1.3 us (2%)
    pallas_call x1, Pallas kernels, team(): pl.pallas_call(functools.partial(team_kernel, lanes), out_shape=jax.Shape...  64.7 us
    unnamed x1, local copies, waits for them, and re-layouts  1.67 us

profile of v3, /device:TPU:0, one launch (start us, length us, event | category | flops | bytes accessed | tf_op | source)
XLA Modules:
  0.0 67.7 jit_solution(15163430605648887152)
XLA Ops:
  0.0 1.3 %select_reduce_fusion = f32[8,128]{1,0:T(8,128)} fusion(f32[128,4]{0,1:T(4,128)} %param.7, s32[128,4]{0,1:T(4,128)} %param.6), kind=kLoop, calls=%fused_computation | loop fusion | flops 11264 | bytes 8192 | tf_op jit(solution)/shard_map/reduce_sum | solution.py:275
  1.3 64.7 %shard_map.55 = bf16[128,1024]{1,0:T(8,128)(2,1)} custom-call(bf16[128,1024]{1,0:T(8,128)(2,1)} %latent_ref.1, f32[8,1,128]{2,1,0:T(1,128)} %bitcast.5, bf16[1,1344,1024]{2,1,0:T(8,128)(2,1)} %bitcast.3, bf16[1,1344,1024]{2,1,0:T(8,128)(2,1)} %bitcast.4), custom_call_target="tpu_custom_call" | custom-call | tf_op jit(solution)/shard_map/pallas_call | solution.py:279
  66.1 1.7 %copy.9 = bf16[128,1024]{1,0:T(8,128)(2,1)} copy(bf16[128,1024]{1,0:T(8,128)(2,1)} %shard_map.55) | data formatting | bytes 524288

commit v4 on v3

--- a/solution.py
+++ b/solution.py
@@ -8,6 +8,7 @@
 from jax.sharding import PartitionSpec as P
 
 CORES = 2
+PIECES = 2
 VMEM_MOST = 60 * 1024 * 1024
 F32, BF16 = jnp.float32, jnp.bfloat16
 
@@ -66,7 +67,7 @@
     latent_ref, share_ref, up_hbm, down_hbm, out_ref,
     rows, shares, up, down, kept, sib_out, sib_in, x_out, x_in, lane_out, lane_in,
     w_sem, lane_s, lane_r, x_s, x_r, sib_s, sib_r,
-    rsib_s, rsib_r, rx_s, rx_r, rlane_s, rlane_r,
+    rsib_s, rsib_r, rx_s, rx_r, rlane_s, rlane_r, next_s, mid_r, lane_mid, lane_sum,
 ):
     tokens = latent_ref.shape[0]
     me = lax.axis_index("expert")
@@ -114,6 +115,15 @@
         return send(src, boxes[kind].at[1, step, 0], x_s.at[kind, step],
                     x_r.at[kind, step], partner)
 
+    around = 2 * jnp.where(inner, 1, 0)
+
+    def crossing(step):
+        return jnp.where(inner & (step == 1), 3, step)
+
+    def to_next(kind):
+        return send(boxes[kind].at[1, around, 0], boxes[kind].at[1, around + 1, 0],
+                    next_s.at[kind], x_r.at[kind, around + 1], lane_peer(1))
+
     def to_sibling(kind, other, step, src=None):
         src = boxes[kind].at[other, step, 0] if src is None else src
         return send(src, boxes[kind].at[other, step, 1], sib_s.at[kind, other, step],
@@ -123,12 +133,21 @@
         return send(sib_out.at[other, step], sib_in.at[other, step], rsib_s.at[other, step],
                     rsib_r.at[other, step], sibling)
 
-    def back_sub(step):
-        return send(x_out.at[step], x_in.at[step], rx_s.at[step], rx_r.at[step], partner)
-
-    def back_lane(step):
-        return send(lane_out.at[step], lane_in.at[step], rlane_s.at[step],
-                    rlane_r.at[step], lane_peer(step))
+    def back_sub(step, piece):
+        return send(x_out.at[step, piece], x_in.at[step, piece], rx_s.at[step, piece],
+                    rx_r.at[step, piece], partner)
+
+    def back_lane(step, piece, src=None):
+        src = lane_out if src is None else src
+        return send(src.at[step, piece], lane_in.at[step, piece],
+                    rlane_s.at[step, piece], rlane_r.at[step, piece], lane_peer(step))
+
+    def to_inner(step, piece):
+        return send(lane_out.at[step, piece], lane_mid.at[5 - step, piece],
+                    rlane_s.at[step, piece], mid_r.at[5 - step, piece], lane_peer(1))
+
+    def span(piece):
+        return pl.ds(piece * (tokens // PIECES), tokens // PIECES)
 
     up_copy = pltpu.make_async_copy(up_hbm.at[0], up, w_sem.at[0])
     down_copy = pltpu.make_async_copy(down_hbm.at[0], down, w_sem.at[1])
@@ -161,9 +180,10 @@
 
     def finish_sub(step):
         back_sibling(1, step).wait_recv()
-        total = kept[1, step] + sib_in[1, step].astype(F32)
-        x_out[step] = total.astype(BF16)
-        back_sub(step).start()
+        for piece in range(PIECES):
+            total = kept[1, step, span(piece)] + sib_in[1, step, span(piece)].astype(F32)
+            x_out[step, piece] = total.astype(BF16)
+            back_sub(step, piece).start()
 
     def gate_column(other, step, side):
         line = shares[other, step, side, me]
@@ -199,13 +219,22 @@
                 for kind in (0, 1):
                     to_lane(kind, step + 1).wait_recv()
             for kind in (0, 1):
-                to_sub(kind, step + 1).start()
+                if relay:
+                    @pl.when(step < 2)
+                    def _():
+                        to_sub(kind, crossing(step + 1)).start()
+                else:
+                    to_sub(kind, step + 1).start()
                 to_sibling(kind, 0, step + 1).start()
 
         @pl.when(other == 1)
         def _():
             for kind in (0, 1):
                 to_sub(kind, step).wait_recv()
+                if relay:
+                    @pl.when(step == around)
+                    def _():
+                        to_next(kind).start()
                 to_sibling(kind, 1, step).start()
 
         for kind in (0, 1):
@@ -231,32 +260,59 @@
     for step in (*range(min(lanes, 3) - 1, 0, -1), 0) if lanes < 4 else (lanes - 1, 1, 0):
         finish_sub(step)
 
-    def column_total(step):
+    def column_total(step, piece):
+        back_sub(step, piece).wait_recv()
+        total = kept[0, step, span(piece)] + sib_in[0, step, span(piece)].astype(F32)
+        return total + x_in[step, piece].astype(F32)
+
+    for step in range(lanes):
         back_sibling(0, step).wait_recv()
-        back_sub(step).wait_recv()
-        return kept[0, step] + sib_in[0, step].astype(F32) + x_in[step].astype(F32)
+    def returned(step, piece):
+        if not relay or step == 1:
+            back_lane(step, piece).start()
+            return
+
+        @pl.when(inner)
+        def _():
+            to_inner(5 - step, piece).wait_recv()
+            total = lane_out[step, piece].astype(F32) + lane_mid[step, piece].astype(F32)
+            lane_sum[step, piece] = total.astype(BF16)
+            back_lane(step, piece, lane_sum).start()
+
+        @pl.when(jnp.logical_not(inner))
+        def _():
+            to_inner(step, piece).start()
 
     for step in (*range(2, lanes), 1) if lanes > 1 else ():
-        lane_out[step] = column_total(step).astype(BF16)
-        back_lane(step).start()
-    total = column_total(0)
-    for step in range(1, lanes):
-        back_lane(step).wait_recv()
-        total = total + lane_in[step].astype(F32)
-    out_ref[...] = total.astype(BF16)
+        for piece in range(PIECES):
+            lane_out[step, piece] = column_total(step, piece).astype(BF16)
+            returned(step, piece)
+    near = 2 + jnp.where(inner, 1, 0)
+    for piece in range(PIECES):
+        total = column_total(0, piece)
+        for step in (1, near) if relay else range(1, lanes):
+            back_lane(step, piece).wait_recv()
+            total = total + lane_in[step, piece].astype(F32)
+        out_ref[span(piece), :] = total.astype(BF16)
 
     for step in range(lanes):
         for kind in (0, 1):
-            to_sub(kind, step).wait_send()
+            if not relay:
+                to_sub(kind, step).wait_send()
+            elif step < 3:
+                to_sub(kind, crossing(step)).wait_send()
+            else:
+                to_next(kind).wait_send()
             for other in (0, 1):
                 to_sibling(kind, other, step).wait_send()
             if step == 1 or (step and not relay):
                 to_lane(kind, step).wait_send()
         for other in (0, 1):
             back_sibling(other, step).wait_send()
-        back_sub(step).wait_send()
-        if step:
-            back_lane(step).wait_send()
+        for piece in range(PIECES):
+            back_sub(step, piece).wait_send()
+            if step:
+                back_lane(step, piece).wait_send()
     if relay:
         @pl.when(inner)
         def _():
@@ -289,15 +345,19 @@
             pltpu.VMEM((2, lanes, tokens, width), F32),
             pltpu.VMEM((2, lanes, tokens, width), BF16),
             pltpu.VMEM((2, lanes, tokens, width), BF16),
-            pltpu.VMEM((lanes, tokens, width), BF16),
-            pltpu.VMEM((lanes, tokens, width), BF16),
-            pltpu.VMEM((lanes, tokens, width), BF16),
-            pltpu.VMEM((lanes, tokens, width), BF16),
+            pltpu.VMEM((lanes, PIECES, tokens // PIECES, width), BF16),
+            pltpu.VMEM((lanes, PIECES, tokens // PIECES, width), BF16),
+            pltpu.VMEM((lanes, PIECES, tokens // PIECES, width), BF16),
+            pltpu.VMEM((lanes, PIECES, tokens // PIECES, width), BF16),
             dma((2,)),
             dma((2, lanes + 2)), dma((2, lanes)), dma((2, lanes)), dma((2, lanes)),
             dma((2, 2, lanes)), dma((2, 2, lanes)),
             dma((2, lanes)), dma((2, lanes)),
-            dma((lanes,)), dma((lanes,)), dma((lanes,)), dma((lanes,)),
+            dma((lanes, PIECES)), dma((lanes, PIECES)), dma((lanes, PIECES)), dma((lanes, PIECES)),
+            dma((2,)),
+            dma((lanes, PIECES)),
+            pltpu.VMEM((lanes, PIECES, tokens // PIECES, width), BF16),
+            pltpu.VMEM((lanes, PIECES, tokens // PIECES, width), BF16),
         ],
         compiler_params=pltpu.CompilerParams(
             collective_id=0, has_side_effects=True, vmem_limit_bytes=VMEM_MOST

time: 67.9 us -> 66 us (0.972)
  Pallas kernels: 64.7 us -> 62.9 us
    pallas_call x1, Pallas kernels: 64.7 us -> 62.9 us  [team(): pl.pallas_call(functools.partial(team_kernel, lanes), out_shape=jax.Shape...]
where the time goes in v4:
time: 66 us; the launch traced here: 65.8 us
  Pallas kernels  62.9 us (95%)
  local copies, waits for them, and re-layouts  1.67 us (3%)
  other arithmetic  1.3 us (2%)
    pallas_call x1, Pallas kernels, team(): pl.pallas_call(functools.partial(team_kernel, lanes), out_shape=jax.Shape...  62.9 us
    unnamed x1, local copies, waits for them, and re-layouts  1.67 us

profile of v4, /device:TPU:0, one launch (start us, length us, event | category | flops | bytes accessed | tf_op | source)
XLA Modules:
  0.0 65.8 jit_solution(9391852750029788177)
XLA Ops:
  0.0 1.3 %select_reduce_fusion = f32[8,128]{1,0:T(8,128)} fusion(f32[128,4]{0,1:T(4,128)} %param.7, s32[128,4]{0,1:T(4,128)} %param.6), kind=kLoop, calls=%fused_computation | loop fusion | flops 11264 | bytes 8192 | tf_op jit(solution)/shard_map/reduce_sum | solution.py:331
  1.3 62.9 %shard_map.55 = bf16[128,1024]{1,0:T(8,128)(2,1)} custom-call(bf16[128,1024]{1,0:T(8,128)(2,1)} %latent_ref.1, f32[8,1,128]{2,1,0:T(1,128)} %bitcast.5, bf16[1,1344,1024]{2,1,0:T(8,128)(2,1)} %bitcast.3, bf16[1,1344,1024]{2,1,0:T(8,128)(2,1)} %bitcast.4), custom_call_target="tpu_custom_call" | custom-call | tf_op jit(solution)/shard_map/pallas_call | solution.py:335
  64.2 1.7 %copy.9 = bf16[128,1024]{1,0:T(8,128)(2,1)} copy(bf16[128,1024]{1,0:T(8,128)(2,1)} %shard_map.55) | data formatting | bytes 524288
